TPU v7x, 512 devices: a whole 4x8x8 slice. The times are simulated.
512 devices in a mesh: group: 64 (over x, y_lo, z), member: 8 (over y_hi, core).
Axes of the slice: x: 4, y: 8 (y_hi: 4, y_lo: 2; y = y_hi * 2 + y_lo), z: 8, core: 2. Of those that a mesh axis runs over, the one named last changes fastest.
Arguments:
- load: float32 [512, 16, 768], P(('group', 'member')), may hold values from -6 to 6
- stiffness: bfloat16 [512, 768, 1024], P(('group', 'member')), as said below
- block_inverse: bfloat16 [512, 768, 1024], P(('group', 'member')), as said below
- deflation: bfloat16 [512, 32, 1024], P(('group', 'member')), may hold values from -0.375 to 0.375
- margin_rows: int32 [512, 4, 64], P(('group', 'member')), may hold values from 0 to 767
- coarse_inverse: bfloat16 [256, 64, 16384], P('member', None, 'group'), as said below
Outputs:
- solution: float32 [512, 16, 768], P(('group', 'member'))
- residual: float32 [512, 16, 768], P(('group', 'member'))
Inputs may be any that keep to these rules, and one draw needn't show every extreme that they name: `margin_rows`: row numbers may repeat within a list. `stiffness`: each row's entry in the column of its own unknown (column i for row i) is the largest entry of the row in magnitude. `block_inverse`: each row's entry in the column of its own unknown is the largest entry of the row in magnitude. `coarse_inverse`: entry [l, h, j] with h * 256 + l == j is the largest entry of its row in magnitude.
All inputs are finite; a program needn't handle non-finite values.
Results may differ from a plain program's by a relative error of at most 0.0085.
Values may be sent and summed in bfloat16 or wider, within the bound.
No kernel may reach another device: no remote copies, remote signals or barrier semaphores. Data moves between devices by JAX's collectives and lax.ppermute only.
A program may use at most 64 MiB of HBM per device.

v0:
```python
import jax
import jax.numpy as jnp
from jax import lax
from jax.sharding import PartitionSpec as P

ITERS = 2


def from_behind(shard, axis, by):
    peers = lax.axis_size(axis)
    return lax.ppermute(shard, axis, [(i, (i + by) % peers) for i in range(peers)])


def local(load, stiffness, block_inverse, deflation, margin_rows, coarse_inverse):
    own_load = load[0]
    stiff_rows = stiffness[0]
    inverse_rows = block_inverse[0]
    basis_rows = deflation[0]
    own_lists = margin_rows[0]
    owned_count = own_load.shape[1]

    def extend(values):
        from_group_lower = from_behind(values, "group", 1)
        from_group_upper = from_behind(values, "group", -1)
        from_member_lower = from_behind(values, "member", 1)
        from_member_upper = from_behind(values, "member", -1)
        pieces = [
            jnp.take(from_group_lower, own_lists[0], axis=1),
            jnp.take(from_group_upper, own_lists[1], axis=1),
            jnp.take(from_member_lower, own_lists[2], axis=1),
            jnp.take(from_member_upper, own_lists[3], axis=1),
        ]
        return jnp.concatenate([values] + pieces, axis=1)

    solution = jnp.zeros_like(own_load)
    residual = own_load
    for step_index in range(ITERS):
        block_values = extend(residual.astype(jnp.bfloat16))
        own_coef = jnp.einsum(
            "cn,kn->ck", block_values, basis_rows, preferred_element_type=jnp.float32
        ).astype(jnp.bfloat16)
        gathered = lax.all_gather(own_coef, "member", axis=1, tiled=True)
        shares = jnp.einsum(
            "lhj,cj->hcl", coarse_inverse, gathered, preferred_element_type=jnp.float32
        )
        arrived = lax.all_to_all(shares, "group", 0, 0, tiled=True)
        prolong = jnp.sum(arrived, axis=0).astype(jnp.bfloat16)
        local_fix = jnp.einsum(
            "cn,un->cu", block_values, inverse_rows, preferred_element_type=jnp.float32
        )
        correction = local_fix + jnp.dot(
            prolong, basis_rows[:, :owned_count], preferred_element_type=jnp.float32
        )
        solution = solution + correction
        solution_block = extend(solution.astype(jnp.bfloat16))
        applied = jnp.einsum(
            "cn,un->cu", solution_block, stiff_rows, preferred_element_type=jnp.float32
        )
        residual = own_load - applied
    return (solution[None], residual[None])


def solution(mesh):
    placed = (
        P(("group", "member"), None, None),
        P(("group", "member"), None, None),
        P(("group", "member"), None, None),
        P(("group", "member"), None, None),
        P(("group", "member"), None, None),
        P("member", None, "group"),
    )
    return jax.shard_map(
        local,
        mesh=mesh,
        in_specs=placed,
        out_specs=(P(("group", "member"), None, None), P(("group", "member"), None, None)),
        check_vma=False,
    )
```

profile of v0, /device:TPU:17, one launch (start us, length us, event | category | flops | bytes accessed | tf_op | source)
XLA Modules:
  0.0 184.7 jit_solution(14538968554219266176)
XLA Ops:
  1.6 2.6 %collective-permute-start.3 = (bf16[16,768]{1,0:T(8,128)(2,1)S(1)}, bf16[16,768]{1,0:T(8,128)(2,1)S(1)}, u32[]{:S(2)}, u32[]{:S(2)}) collective-permute-start(bf16[16,768]{1,0:T(8,128)(2,1)S(1)} %bitcast_convert_fusion), channel_id=1, source_target_pairs={{0,7},{1,0},{2,1},{3,2},{4,3},{5,4},{6,5},{7,6},{8,15},{9,8},{10,9... | collective-permute-start | bytes 73736 | tf_op jit(solution)/shard_map/ppermute | solution.py:11
  4.2 5.3 %collective-permute-start.2 = (bf16[16,768]{1,0:T(8,128)(2,1)S(1)}, bf16[16,768]{1,0:T(8,128)(2,1)S(1)}, u32[]{:S(2)}, u32[]{:S(2)}) collective-permute-start(bf16[16,768]{1,0:T(8,128)(2,1)S(1)} %bitcast_convert_fusion), channel_id=1, source_target_pairs={{0,1},{1,2},{2,3},{3,4},{4,5},{5,6},{6,7},{7,0},{8,9},{9,10},{10,1... | collective-permute-start | bytes 73736 | tf_op jit(solution)/shard_map/ppermute | solution.py:11
  9.5 13.6 %collective-permute-start.1 = (bf16[16,768]{1,0:T(8,128)(2,1)S(1)}, bf16[16,768]{1,0:T(8,128)(2,1)S(1)}, u32[]{:S(2)}, u32[]{:S(2)}) collective-permute-start(bf16[16,768]{1,0:T(8,128)(2,1)S(1)} %bitcast_convert_fusion), channel_id=1, source_target_pairs={{0,504},{8,0},{16,8},{24,16},{32,24},{40,32},{48,40},{56,48},{64,5... | collective-permute-start | bytes 73736 | tf_op jit(solution)/shard_map/ppermute | solution.py:11
  23.2 1.9 %collective-permute-start = (bf16[16,768]{1,0:T(8,128)(2,1)S(1)}, bf16[16,768]{1,0:T(8,128)(2,1)S(1)}, u32[]{:S(2)}, u32[]{:S(2)}) collective-permute-start(bf16[16,768]{1,0:T(8,128)(2,1)S(1)} %bitcast_convert_fusion), channel_id=1, source_target_pairs={{0,8},{8,16},{16,24},{24,32},{32,40},{40,48},{48,56},{56,64},{64,7... | collective-permute-start | bytes 73736 | tf_op jit(solution)/shard_map/ppermute | solution.py:11
  26.1 5.9 %collective-permute-done = bf16[16,768]{1,0:T(8,128)(2,1)S(1)} collective-permute-done((bf16[16,768]{1,0:T(8,128)(2,1)S(1)}, bf16[16,768]{1,0:T(8,128)(2,1)S(1)}, u32[]{:S(2)}, u32[]{:S(2)}) %collective-permute-start) | collective-permute-done | bytes 24608 | tf_op jit(solution)/shard_map/ppermute | solution.py:11
  36.7 13.9 %all-gather = bf16[8,32,16]{1,2,0:T(8,128)(2,1)S(1)} all-gather(bf16[1,32,16]{1,2,0:T(8,128)(2,1)S(1)} %fusion.29), channel_id=1, replica_groups=mesh['group'=64,'member'=8] {'member'}, dimensions={0}, use_global_device_ids=true | all-gather | bytes 9216 | tf_op jit(solution)/shard_map/all_gather | solution.py:42
  51.8 13.7 %all_to_all.10 = f32[64,1,512]{2,1,0:T(1,128)S(1)} all-to-all(f32[64,1,512]{2,1,0:T(1,128)S(1)} %reshape.201), channel_id=1, replica_groups=mesh['group'=64,'member'=8] {'group'}, dimensions={0} | all-to-all | bytes 262144 | tf_op jit(solution)/shard_map/all_to_all | solution.py:46
  68.4 2.2 %collective-permute-start.4 = (bf16[16,768]{1,0:T(8,128)(2,1)S(1)}, bf16[16,768]{1,0:T(8,128)(2,1)}, u32[]{:S(2)}, u32[]{:S(2)}) collective-permute-start(bf16[16,768]{1,0:T(8,128)(2,1)S(1)} %get-tuple-element.17), channel_id=1, source_target_pairs={{0,8},{8,16},{16,24},{24,32},{32,40},{40,48},{48,56},{56,64},{64,7... | collective-permute-start | bytes 73736 | tf_op jit(solution)/shard_map/ppermute | solution.py:11
  70.7 3.9 %collective-permute-start.7 = (bf16[16,768]{1,0:T(8,128)(2,1)S(1)}, bf16[16,768]{1,0:T(8,128)(2,1)S(1)}, u32[]{:S(2)}, u32[]{:S(2)}) collective-permute-start(bf16[16,768]{1,0:T(8,128)(2,1)S(1)} %get-tuple-element.17), channel_id=1, source_target_pairs={{0,7},{1,0},{2,1},{3,2},{4,3},{5,4},{6,5},{7,6},{8,15},{9,8},{10,9... | collective-permute-start | bytes 73736 | tf_op jit(solution)/shard_map/ppermute | solution.py:11
  74.6 4.0 %collective-permute-start.6 = (bf16[16,768]{1,0:T(8,128)(2,1)S(1)}, bf16[16,768]{1,0:T(8,128)(2,1)S(1)}, u32[]{:S(2)}, u32[]{:S(2)}) collective-permute-start(bf16[16,768]{1,0:T(8,128)(2,1)S(1)} %get-tuple-element.17), channel_id=1, source_target_pairs={{0,1},{1,2},{2,3},{3,4},{4,5},{5,6},{6,7},{7,0},{8,9},{9,10},{10,1... | collective-permute-start | bytes 73736 | tf_op jit(solution)/shard_map/ppermute | solution.py:11
  78.6 7.1 %collective-permute-start.5 = (bf16[16,768]{1,0:T(8,128)(2,1)S(1)}, bf16[16,768]{1,0:T(8,128)(2,1)}, u32[]{:S(2)}, u32[]{:S(2)}) collective-permute-start(bf16[16,768]{1,0:T(8,128)(2,1)S(1)} %get-tuple-element.17), channel_id=1, source_target_pairs={{0,504},{8,0},{16,8},{24,16},{32,24},{40,32},{48,40},{56,48},{64,5... | collective-permute-start | bytes 73736 | tf_op jit(solution)/shard_map/ppermute | solution.py:11
  93.7 1.9 %collective-permute-start.8 = (bf16[16,768]{1,0:T(8,128)(2,1)S(1)}, bf16[16,768]{1,0:T(8,128)(2,1)}, u32[]{:S(2)}, u32[]{:S(2)}) collective-permute-start(bf16[16,768]{1,0:T(8,128)(2,1)S(1)} %fusion.26), channel_id=1, source_target_pairs={{0,8},{8,16},{16,24},{24,32},{32,40},{40,48},{48,56},{56,64},{64,7... | collective-permute-start | bytes 73736 | tf_op jit(solution)/shard_map/ppermute | solution.py:11
  95.6 1.9 %collective-permute-start.11 = (bf16[16,768]{1,0:T(8,128)(2,1)S(1)}, bf16[16,768]{1,0:T(8,128)(2,1)S(1)}, u32[]{:S(2)}, u32[]{:S(2)}) collective-permute-start(bf16[16,768]{1,0:T(8,128)(2,1)S(1)} %fusion.26), channel_id=1, source_target_pairs={{0,7},{1,0},{2,1},{3,2},{4,3},{5,4},{6,5},{7,6},{8,15},{9,8},{10,9... | collective-permute-start | bytes 73736 | tf_op jit(solution)/shard_map/ppermute | solution.py:11
  97.5 5.8 %collective-permute-start.10 = (bf16[16,768]{1,0:T(8,128)(2,1)S(1)}, bf16[16,768]{1,0:T(8,128)(2,1)S(1)}, u32[]{:S(2)}, u32[]{:S(2)}) collective-permute-start(bf16[16,768]{1,0:T(8,128)(2,1)S(1)} %fusion.26), channel_id=1, source_target_pairs={{0,1},{1,2},{2,3},{3,4},{4,5},{5,6},{6,7},{7,0},{8,9},{9,10},{10,1... | collective-permute-start | bytes 73736 | tf_op jit(solution)/shard_map/ppermute | solution.py:11
  103.3 7.6 %collective-permute-start.9 = (bf16[16,768]{1,0:T(8,128)(2,1)S(1)}, bf16[16,768]{1,0:T(8,128)(2,1)}, u32[]{:S(2)}, u32[]{:S(2)}) collective-permute-start(bf16[16,768]{1,0:T(8,128)(2,1)S(1)} %fusion.26), channel_id=1, source_target_pairs={{0,504},{8,0},{16,8},{24,16},{32,24},{40,32},{48,40},{56,48},{64,5... | collective-permute-start | bytes 73736 | tf_op jit(solution)/shard_map/ppermute | solution.py:11
  118.6 11.8 %all-gather.1 = bf16[8,32,16]{1,2,0:T(8,128)(2,1)S(1)} all-gather(bf16[1,32,16]{1,2,0:T(8,128)(2,1)S(1)} %fusion.30), channel_id=1, replica_groups=mesh['group'=64,'member'=8] {'member'}, dimensions={0}, use_global_device_ids=true | all-gather | bytes 9216 | tf_op jit(solution)/shard_map/all_gather | solution.py:42
  131.1 1.7 convolution_bitcast_fusion
  135.3 17.8 %all_to_all.11 = f32[64,1,512]{2,1,0:T(1,128)S(1)} all-to-all(f32[64,1,512]{2,1,0:T(1,128)S(1)} %reshape.203), channel_id=1, replica_groups=mesh['group'=64,'member'=8] {'group'}, dimensions={0} | all-to-all | bytes 262144 | tf_op jit(solution)/shard_map/all_to_all | solution.py:46
  156.2 1.9 %fusion.40 = (bf16[16,768]{1,0:T(8,128)(2,1)S(1)}, f32[16,768]{1,0:T(8,128)}) fusion(f32[16,768]{1,0:T(8,128)} %get-tuple-element.18, f32[16,768]{1,0:T(8,128)S(1)} %fusion.31, bf16[16,1024]{1,0:T(8,128)(2,1)S(1)} %concatenate.14, bf16[1,768,1024]{2,1,0:T(8,128)(2,1)S(1)} %copy-done), kind=kOutput, calls=%fused_computation.75 | convolution fusion | flops 25202688 | bytes 1777664 | tf_op jit(solution)/shard_map/cn,un->cu/dot_general | solution.py:48
  158.1 2.5 %collective-permute-start.12 = (bf16[16,768]{1,0:T(8,128)(2,1)S(1)}, bf16[16,768]{1,0:T(8,128)(2,1)S(1)}, u32[]{:S(2)}, u32[]{:S(2)}) collective-permute-start(bf16[16,768]{1,0:T(8,128)(2,1)S(1)} %get-tuple-element.19), channel_id=1, source_target_pairs={{0,8},{8,16},{16,24},{24,32},{32,40},{40,48},{48,56},{56,64},{64,7... | collective-permute-start | bytes 73736 | tf_op jit(solution)/shard_map/ppermute | solution.py:11
  160.6 7.0 %collective-permute-start.13 = (bf16[16,768]{1,0:T(8,128)(2,1)S(1)}, bf16[16,768]{1,0:T(8,128)(2,1)S(1)}, u32[]{:S(2)}, u32[]{:S(2)}) collective-permute-start(bf16[16,768]{1,0:T(8,128)(2,1)S(1)} %get-tuple-element.19), channel_id=1, source_target_pairs={{0,504},{8,0},{16,8},{24,16},{32,24},{40,32},{48,40},{56,48},{64,5... | collective-permute-start | bytes 73736 | tf_op jit(solution)/shard_map/ppermute | solution.py:11
  167.6 7.5 %collective-permute-start.14 = (bf16[16,768]{1,0:T(8,128)(2,1)S(1)}, bf16[16,768]{1,0:T(8,128)(2,1)S(1)}, u32[]{:S(2)}, u32[]{:S(2)}) collective-permute-start(bf16[16,768]{1,0:T(8,128)(2,1)S(1)} %get-tuple-element.19), channel_id=1, source_target_pairs={{0,1},{1,2},{2,3},{3,4},{4,5},{5,6},{6,7},{7,0},{8,9},{9,10},{10,1... | collective-permute-start | bytes 73736 | tf_op jit(solution)/shard_map/ppermute | solution.py:11
  175.1 1.9 %collective-permute-start.15 = (bf16[16,768]{1,0:T(8,128)(2,1)S(1)}, bf16[16,768]{1,0:T(8,128)(2,1)S(1)}, u32[]{:S(2)}, u32[]{:S(2)}) collective-permute-start(bf16[16,768]{1,0:T(8,128)(2,1)S(1)} %get-tuple-element.19), channel_id=1, source_target_pairs={{0,7},{1,0},{2,1},{3,2},{4,3},{5,4},{6,5},{7,6},{8,15},{9,8},{10,9... | collective-permute-start | bytes 73736 | tf_op jit(solution)/shard_map/ppermute | solution.py:11
  180.1 2.3 %collective-permute-done.15 = bf16[16,768]{1,0:T(8,128)(2,1)S(1)} collective-permute-done((bf16[16,768]{1,0:T(8,128)(2,1)S(1)}, bf16[16,768]{1,0:T(8,128)(2,1)S(1)}, u32[]{:S(2)}, u32[]{:S(2)}) %collective-permute-start.15) | collective-permute-done | bytes 24608 | tf_op jit(solution)/shard_map/ppermute | solution.py:11
  (145 shorter events, 37.7 us)
Async XLA Ops:
  0.6 66.6 %copy-start = (bf16[1,768,1024]{2,1,0:T(8,128)(2,1)S(1)}, bf16[1,768,1024]{2,1,0:T(8,128)(2,1)}, u32[]{:S(2)}) copy-start(bf16[1,768,1024]{2,1,0:T(8,128)(2,1)} %param.10) | copy-start | bytes 4718596
  0.6 50.0 %copy-start.2 = (bf16[32,64,256]{2,1,0:T(8,128)(2,1)S(1)}, bf16[32,64,256]{2,1,0:T(8,128)(2,1)}, u32[]{:S(2)}) copy-start(bf16[32,64,256]{2,1,0:T(8,128)(2,1)} %param.13) | copy-start | bytes 3145732
  1.6 33.0 %collective-permute-start.3 = (bf16[16,768]{1,0:T(8,128)(2,1)S(1)}, bf16[16,768]{1,0:T(8,128)(2,1)S(1)}, u32[]{:S(2)}, u32[]{:S(2)}) collective-permute-start(bf16[16,768]{1,0:T(8,128)(2,1)S(1)} %bitcast_convert_fusion), channel_id=1, source_target_pairs={{0,7},{1,0},{2,1},{3,2},{4,3},{5,4},{6,5},{7,6},{8,15},{9,8},{10,9... | collective-permute-start | bytes 73736 | tf_op jit(solution)/shard_map/ppermute | solution.py:11
  4.2 29.6 %collective-permute-start.2 = (bf16[16,768]{1,0:T(8,128)(2,1)S(1)}, bf16[16,768]{1,0:T(8,128)(2,1)S(1)}, u32[]{:S(2)}, u32[]{:S(2)}) collective-permute-start(bf16[16,768]{1,0:T(8,128)(2,1)S(1)} %bitcast_convert_fusion), channel_id=1, source_target_pairs={{0,1},{1,2},{2,3},{3,4},{4,5},{5,6},{6,7},{7,0},{8,9},{9,10},{10,1... | collective-permute-start | bytes 73736 | tf_op jit(solution)/shard_map/ppermute | solution.py:11
  9.5 23.3 %collective-permute-start.1 = (bf16[16,768]{1,0:T(8,128)(2,1)S(1)}, bf16[16,768]{1,0:T(8,128)(2,1)S(1)}, u32[]{:S(2)}, u32[]{:S(2)}) collective-permute-start(bf16[16,768]{1,0:T(8,128)(2,1)S(1)} %bitcast_convert_fusion), channel_id=1, source_target_pairs={{0,504},{8,0},{16,8},{24,16},{32,24},{40,32},{48,40},{56,48},{64,5... | collective-permute-start | bytes 73736 | tf_op jit(solution)/shard_map/ppermute | solution.py:11
  23.2 8.8 %collective-permute-start = (bf16[16,768]{1,0:T(8,128)(2,1)S(1)}, bf16[16,768]{1,0:T(8,128)(2,1)S(1)}, u32[]{:S(2)}, u32[]{:S(2)}) collective-permute-start(bf16[16,768]{1,0:T(8,128)(2,1)S(1)} %bitcast_convert_fusion), channel_id=1, source_target_pairs={{0,8},{8,16},{16,24},{24,32},{32,40},{40,48},{48,56},{56,64},{64,7... | collective-permute-start | bytes 73736 | tf_op jit(solution)/shard_map/ppermute | solution.py:11
  26.0 61.3 %copy-start.11 = (pred[64]{0:T(512)(128)(4,1)}, pred[64]{0:T(512)(128)(4,1)S(1)}, u32[]{:S(2)}) copy-start(pred[64]{0:T(512)(128)(4,1)S(1)} %get-tuple-element.13) | copy-start | bytes 196
  26.0 60.5 %copy-start.17 = (s32[1024]{0:T(1024)}, s32[1024]{0:T(1024)S(1)}, u32[]{:S(2)}) copy-start(s32[1024]{0:T(1024)S(1)} %pad_clamp_fusion.3) | copy-start | bytes 12292
  68.4 17.3 %collective-permute-start.4 = (bf16[16,768]{1,0:T(8,128)(2,1)S(1)}, bf16[16,768]{1,0:T(8,128)(2,1)}, u32[]{:S(2)}, u32[]{:S(2)}) collective-permute-start(bf16[16,768]{1,0:T(8,128)(2,1)S(1)} %get-tuple-element.17), channel_id=1, source_target_pairs={{0,8},{8,16},{16,24},{24,32},{32,40},{40,48},{48,56},{56,64},{64,7... | collective-permute-start | bytes 73736 | tf_op jit(solution)/shard_map/ppermute | solution.py:11
  70.7 20.8 %collective-permute-start.7 = (bf16[16,768]{1,0:T(8,128)(2,1)S(1)}, bf16[16,768]{1,0:T(8,128)(2,1)S(1)}, u32[]{:S(2)}, u32[]{:S(2)}) collective-permute-start(bf16[16,768]{1,0:T(8,128)(2,1)S(1)} %get-tuple-element.17), channel_id=1, source_target_pairs={{0,7},{1,0},{2,1},{3,2},{4,3},{5,4},{6,5},{7,6},{8,15},{9,8},{10,9... | collective-permute-start | bytes 73736 | tf_op jit(solution)/shard_map/ppermute | solution.py:11
  74.6 15.1 %collective-permute-start.6 = (bf16[16,768]{1,0:T(8,128)(2,1)S(1)}, bf16[16,768]{1,0:T(8,128)(2,1)S(1)}, u32[]{:S(2)}, u32[]{:S(2)}) collective-permute-start(bf16[16,768]{1,0:T(8,128)(2,1)S(1)} %get-tuple-element.17), channel_id=1, source_target_pairs={{0,1},{1,2},{2,3},{3,4},{4,5},{5,6},{6,7},{7,0},{8,9},{9,10},{10,1... | collective-permute-start | bytes 73736 | tf_op jit(solution)/shard_map/ppermute | solution.py:11
  78.6 8.7 %collective-permute-start.5 = (bf16[16,768]{1,0:T(8,128)(2,1)S(1)}, bf16[16,768]{1,0:T(8,128)(2,1)}, u32[]{:S(2)}, u32[]{:S(2)}) collective-permute-start(bf16[16,768]{1,0:T(8,128)(2,1)S(1)} %get-tuple-element.17), channel_id=1, source_target_pairs={{0,504},{8,0},{16,8},{24,16},{32,24},{40,32},{48,40},{56,48},{64,5... | collective-permute-start | bytes 73736 | tf_op jit(solution)/shard_map/ppermute | solution.py:11
  93.7 17.2 %collective-permute-start.8 = (bf16[16,768]{1,0:T(8,128)(2,1)S(1)}, bf16[16,768]{1,0:T(8,128)(2,1)}, u32[]{:S(2)}, u32[]{:S(2)}) collective-permute-start(bf16[16,768]{1,0:T(8,128)(2,1)S(1)} %fusion.26), channel_id=1, source_target_pairs={{0,8},{8,16},{16,24},{24,32},{32,40},{40,48},{48,56},{56,64},{64,7... | collective-permute-start | bytes 73736 | tf_op jit(solution)/shard_map/ppermute | solution.py:11
  95.6 21.2 %collective-permute-start.11 = (bf16[16,768]{1,0:T(8,128)(2,1)S(1)}, bf16[16,768]{1,0:T(8,128)(2,1)S(1)}, u32[]{:S(2)}, u32[]{:S(2)}) collective-permute-start(bf16[16,768]{1,0:T(8,128)(2,1)S(1)} %fusion.26), channel_id=1, source_target_pairs={{0,7},{1,0},{2,1},{3,2},{4,3},{5,4},{6,5},{7,6},{8,15},{9,8},{10,9... | collective-permute-start | bytes 73736 | tf_op jit(solution)/shard_map/ppermute | solution.py:11
  97.5 17.5 %collective-permute-start.10 = (bf16[16,768]{1,0:T(8,128)(2,1)S(1)}, bf16[16,768]{1,0:T(8,128)(2,1)S(1)}, u32[]{:S(2)}, u32[]{:S(2)}) collective-permute-start(bf16[16,768]{1,0:T(8,128)(2,1)S(1)} %fusion.26), channel_id=1, source_target_pairs={{0,1},{1,2},{2,3},{3,4},{4,5},{5,6},{6,7},{7,0},{8,9},{9,10},{10,1... | collective-permute-start | bytes 73736 | tf_op jit(solution)/shard_map/ppermute | solution.py:11
  103.3 9.4 %collective-permute-start.9 = (bf16[16,768]{1,0:T(8,128)(2,1)S(1)}, bf16[16,768]{1,0:T(8,128)(2,1)}, u32[]{:S(2)}, u32[]{:S(2)}) collective-permute-start(bf16[16,768]{1,0:T(8,128)(2,1)S(1)} %fusion.26), channel_id=1, source_target_pairs={{0,504},{8,0},{16,8},{24,16},{32,24},{40,32},{48,40},{56,48},{64,5... | collective-permute-start | bytes 73736 | tf_op jit(solution)/shard_map/ppermute | solution.py:11
  156.0 27.4 %copy-start.10 = (pred[64]{0:T(512)(128)(4,1)S(1)}, pred[64]{0:T(512)(128)(4,1)}, u32[]{:S(2)}) copy-start(pred[64]{0:T(512)(128)(4,1)} %copy-done.9) | copy-start | bytes 196
  156.0 27.4 %copy-start.13 = (pred[64]{0:T(512)(128)(4,1)S(1)}, pred[64]{0:T(512)(128)(4,1)}, u32[]{:S(2)}) copy-start(pred[64]{0:T(512)(128)(4,1)} %copy-done.11) | copy-start | bytes 196
  156.1 27.4 %copy-start.6 = (pred[64]{0:T(512)(128)(4,1)S(1)}, pred[64]{0:T(512)(128)(4,1)}, u32[]{:S(2)}) copy-start(pred[64]{0:T(512)(128)(4,1)} %copy-done.5) | copy-start | bytes 196
  156.1 27.4 %copy-start.8 = (pred[64]{0:T(512)(128)(4,1)S(1)}, pred[64]{0:T(512)(128)(4,1)}, u32[]{:S(2)}) copy-start(pred[64]{0:T(512)(128)(4,1)} %copy-done.7) | copy-start | bytes 196
  158.1 18.9 %collective-permute-start.12 = (bf16[16,768]{1,0:T(8,128)(2,1)S(1)}, bf16[16,768]{1,0:T(8,128)(2,1)S(1)}, u32[]{:S(2)}, u32[]{:S(2)}) collective-permute-start(bf16[16,768]{1,0:T(8,128)(2,1)S(1)} %get-tuple-element.19), channel_id=1, source_target_pairs={{0,8},{8,16},{16,24},{24,32},{32,40},{40,48},{48,56},{56,64},{64,7... | collective-permute-start | bytes 73736 | tf_op jit(solution)/shard_map/ppermute | solution.py:11
  160.6 17.4 %collective-permute-start.13 = (bf16[16,768]{1,0:T(8,128)(2,1)S(1)}, bf16[16,768]{1,0:T(8,128)(2,1)S(1)}, u32[]{:S(2)}, u32[]{:S(2)}) collective-permute-start(bf16[16,768]{1,0:T(8,128)(2,1)S(1)} %get-tuple-element.19), channel_id=1, source_target_pairs={{0,504},{8,0},{16,8},{24,16},{32,24},{40,32},{48,40},{56,48},{64,5... | collective-permute-start | bytes 73736 | tf_op jit(solution)/shard_map/ppermute | solution.py:11
  167.6 11.5 %collective-permute-start.14 = (bf16[16,768]{1,0:T(8,128)(2,1)S(1)}, bf16[16,768]{1,0:T(8,128)(2,1)S(1)}, u32[]{:S(2)}, u32[]{:S(2)}) collective-permute-start(bf16[16,768]{1,0:T(8,128)(2,1)S(1)} %get-tuple-element.19), channel_id=1, source_target_pairs={{0,1},{1,2},{2,3},{3,4},{4,5},{5,6},{6,7},{7,0},{8,9},{9,10},{10,1... | collective-permute-start | bytes 73736 | tf_op jit(solution)/shard_map/ppermute | solution.py:11
  175.1 7.3 %collective-permute-start.15 = (bf16[16,768]{1,0:T(8,128)(2,1)S(1)}, bf16[16,768]{1,0:T(8,128)(2,1)S(1)}, u32[]{:S(2)}, u32[]{:S(2)}) collective-permute-start(bf16[16,768]{1,0:T(8,128)(2,1)S(1)} %get-tuple-element.19), channel_id=1, source_target_pairs={{0,7},{1,0},{2,1},{3,2},{4,3},{5,4},{6,5},{7,6},{8,15},{9,8},{10,9... | collective-permute-start | bytes 73736 | tf_op jit(solution)/shard_map/ppermute | solution.py:11
  (10 other events, 240.8 us)
where the time goes:
time: 186 us; the launch traced here: 185 us
  starting transfers between devices  76.7 us (41%)
  blocking collectives  57.2 us (31%)
  local copies, waits for them, and re-layouts  24.3 us (13%)
  other arithmetic  8.75 us (5%)
  matrix products  8.35 us (4%)
  waiting for transfers between devices  8.18 us (4%)
    ppermute x16, starting transfers between devices, from_behind(): lax.ppermute(shard, axis, [(i, (i + by) % peers) for i in range(peers)])  76.7 us
    all_to_all x2, blocking collectives, local(): arrived = lax.all_to_all(shares, 'group', 0, 0, tiled=True)  31.4 us
    all_gather x2, blocking collectives, local(): gathered = lax.all_gather(own_coef, 'member', axis=1, tiled=True)  25.7 us
    ppermute x16, waiting for transfers between devices, from_behind(): lax.ppermute(shard, axis, [(i, (i + by) % peers) for i in range(peers)])  8.18 us
    ppermute x16, local copies, waits for them, and re-layouts, from_behind(): lax.ppermute(shard, axis, [(i, (i + by) % peers) for i in range(peers)])  5.63 us
  transfers between devices with their start and end apart: 16, of which 2 were waited for; matrix products, arithmetic and copies ran while one was open for 10% of the time, Pallas kernels for 0%

commit v1 on v0

--- a/solution.py
+++ b/solution.py
@@ -39,7 +39,9 @@
         own_coef = jnp.einsum(
             "cn,kn->ck", block_values, basis_rows, preferred_element_type=jnp.float32
         ).astype(jnp.bfloat16)
-        gathered = lax.all_gather(own_coef, "member", axis=1, tiled=True)
+        gathered = jnp.concatenate(
+            lax.all_to_all(jnp.stack([own_coef] * lax.axis_size("member")), "member", 0, 0), axis=1
+        )
         shares = jnp.einsum(
             "lhj,cj->hcl", coarse_inverse, gathered, preferred_element_type=jnp.float32
         )

time: 186 us -> 179 us (0.962)
  the two profiles are of different devices: /device:TPU:17 before, /device:TPU:1 now
where the time goes in v1:
time: 179 us; the launch traced here: 177 us
  starting transfers between devices  71.5 us (40%)
  blocking collectives  55.8 us (31%)
  local copies, waits for them, and re-layouts  24.7 us (14%)
  other arithmetic  8.75 us (5%)
  matrix products  8.35 us (5%)
  waiting for transfers between devices  6.99 us (4%)
    ppermute x16, starting transfers between devices, from_behind(): lax.ppermute(shard, axis, [(i, (i + by) % peers) for i in range(peers)])  71.5 us
    all_to_all x2, blocking collectives, local(): arrived = lax.all_to_all(shares, 'group', 0, 0, tiled=True)  30.3 us
    all_to_all x2, blocking collectives, local(): lax.all_to_all(jnp.stack([own_coef] * lax.axis_size('member')), 'member',...  25.5 us
    ppermute x16, waiting for transfers between devices, from_behind(): lax.ppermute(shard, axis, [(i, (i + by) % peers) for i in range(peers)])  6.99 us
    ppermute x16, local copies, waits for them, and re-layouts, from_behind(): lax.ppermute(shard, axis, [(i, (i + by) % peers) for i in range(peers)])  5.63 us
  transfers between devices with their start and end apart: 16, of which 2 were waited for; matrix products, arithmetic and copies ran while one was open for 10% of the time, Pallas kernels for 0%

profile of v1, /device:TPU:1, one launch (start us, length us, event | category | flops | bytes accessed | tf_op | source)
XLA Modules:
  0.0 177.3 jit_solution(16157001726291903450)
XLA Ops:
  1.6 8.7 %collective-permute-start.3 = (bf16[16,768]{1,0:T(8,128)(2,1)S(1)}, bf16[16,768]{1,0:T(8,128)(2,1)S(1)}, u32[]{:S(2)}, u32[]{:S(2)}) collective-permute-start(bf16[16,768]{1,0:T(8,128)(2,1)S(1)} %bitcast_convert_fusion), channel_id=1, source_target_pairs={{0,7},{1,0},{2,1},{3,2},{4,3},{5,4},{6,5},{7,6},{8,15},{9,8},{10,9... | collective-permute-start | bytes 73736 | tf_op jit(solution)/shard_map/ppermute | solution.py:11
  10.4 1.9 %collective-permute-start.2 = (bf16[16,768]{1,0:T(8,128)(2,1)S(1)}, bf16[16,768]{1,0:T(8,128)(2,1)S(1)}, u32[]{:S(2)}, u32[]{:S(2)}) collective-permute-start(bf16[16,768]{1,0:T(8,128)(2,1)S(1)} %bitcast_convert_fusion), channel_id=1, source_target_pairs={{0,1},{1,2},{2,3},{3,4},{4,5},{5,6},{6,7},{7,0},{8,9},{9,10},{10,1... | collective-permute-start | bytes 73736 | tf_op jit(solution)/shard_map/ppermute | solution.py:11
  12.3 10.7 %collective-permute-start.1 = (bf16[16,768]{1,0:T(8,128)(2,1)S(1)}, bf16[16,768]{1,0:T(8,128)(2,1)S(1)}, u32[]{:S(2)}, u32[]{:S(2)}) collective-permute-start(bf16[16,768]{1,0:T(8,128)(2,1)S(1)} %bitcast_convert_fusion), channel_id=1, source_target_pairs={{0,504},{8,0},{16,8},{24,16},{32,24},{40,32},{48,40},{56,48},{64,5... | collective-permute-start | bytes 73736 | tf_op jit(solution)/shard_map/ppermute | solution.py:11
  23.0 1.9 %collective-permute-start = (bf16[16,768]{1,0:T(8,128)(2,1)S(1)}, bf16[16,768]{1,0:T(8,128)(2,1)S(1)}, u32[]{:S(2)}, u32[]{:S(2)}) collective-permute-start(bf16[16,768]{1,0:T(8,128)(2,1)S(1)} %bitcast_convert_fusion), channel_id=1, source_target_pairs={{0,8},{8,16},{16,24},{24,32},{32,40},{40,48},{48,56},{56,64},{64,7... | collective-permute-start | bytes 73736 | tf_op jit(solution)/shard_map/ppermute | solution.py:11
  25.9 5.9 %collective-permute-done = bf16[16,768]{1,0:T(8,128)(2,1)S(1)} collective-permute-done((bf16[16,768]{1,0:T(8,128)(2,1)S(1)}, bf16[16,768]{1,0:T(8,128)(2,1)S(1)}, u32[]{:S(2)}, u32[]{:S(2)}) %collective-permute-start) | collective-permute-done | bytes 24608 | tf_op jit(solution)/shard_map/ppermute | solution.py:11
  36.6 12.9 %all_to_all.20 = bf16[8,2,256]{2,1,0:T(2,128)(2,1)S(1)} all-to-all(bf16[8,2,256]{2,1,0:T(2,128)(2,1)S(1)} %reshape.217), channel_id=1, replica_groups=mesh['group'=64,'member'=8] {'member'}, dimensions={0} | all-to-all | bytes 16384 | tf_op jit(solution)/shard_map/all_to_all | solution.py:43
  50.9 13.4 %all_to_all.21 = f32[64,1,512]{2,1,0:T(1,128)S(1)} all-to-all(f32[64,1,512]{2,1,0:T(1,128)S(1)} %reshape.219), channel_id=1, replica_groups=mesh['group'=64,'member'=8] {'group'}, dimensions={0} | all-to-all | bytes 262144 | tf_op jit(solution)/shard_map/all_to_all | solution.py:48
  67.2 2.5 %collective-permute-start.4 = (bf16[16,768]{1,0:T(8,128)(2,1)S(1)}, bf16[16,768]{1,0:T(8,128)(2,1)}, u32[]{:S(2)}, u32[]{:S(2)}) collective-permute-start(bf16[16,768]{1,0:T(8,128)(2,1)S(1)} %get-tuple-element.17), channel_id=1, source_target_pairs={{0,8},{8,16},{16,24},{24,32},{32,40},{40,48},{48,56},{56,64},{64,7... | collective-permute-start | bytes 73736 | tf_op jit(solution)/shard_map/ppermute | solution.py:11
  69.7 4.1 %collective-permute-start.7 = (bf16[16,768]{1,0:T(8,128)(2,1)S(1)}, bf16[16,768]{1,0:T(8,128)(2,1)S(1)}, u32[]{:S(2)}, u32[]{:S(2)}) collective-permute-start(bf16[16,768]{1,0:T(8,128)(2,1)S(1)} %get-tuple-element.17), channel_id=1, source_target_pairs={{0,7},{1,0},{2,1},{3,2},{4,3},{5,4},{6,5},{7,6},{8,15},{9,8},{10,9... | collective-permute-start | bytes 73736 | tf_op jit(solution)/shard_map/ppermute | solution.py:11
  73.9 2.3 %collective-permute-start.6 = (bf16[16,768]{1,0:T(8,128)(2,1)S(1)}, bf16[16,768]{1,0:T(8,128)(2,1)S(1)}, u32[]{:S(2)}, u32[]{:S(2)}) collective-permute-start(bf16[16,768]{1,0:T(8,128)(2,1)S(1)} %get-tuple-element.17), channel_id=1, source_target_pairs={{0,1},{1,2},{2,3},{3,4},{4,5},{5,6},{6,7},{7,0},{8,9},{9,10},{10,1... | collective-permute-start | bytes 73736 | tf_op jit(solution)/shard_map/ppermute | solution.py:11
  76.2 7.1 %collective-permute-start.5 = (bf16[16,768]{1,0:T(8,128)(2,1)S(1)}, bf16[16,768]{1,0:T(8,128)(2,1)}, u32[]{:S(2)}, u32[]{:S(2)}) collective-permute-start(bf16[16,768]{1,0:T(8,128)(2,1)S(1)} %get-tuple-element.17), channel_id=1, source_target_pairs={{0,504},{8,0},{16,8},{24,16},{32,24},{40,32},{48,40},{56,48},{64,5... | collective-permute-start | bytes 73736 | tf_op jit(solution)/shard_map/ppermute | solution.py:11
  91.3 1.9 %collective-permute-start.8 = (bf16[16,768]{1,0:T(8,128)(2,1)S(1)}, bf16[16,768]{1,0:T(8,128)(2,1)}, u32[]{:S(2)}, u32[]{:S(2)}) collective-permute-start(bf16[16,768]{1,0:T(8,128)(2,1)S(1)} %fusion.26), channel_id=1, source_target_pairs={{0,8},{8,16},{16,24},{24,32},{32,40},{40,48},{48,56},{56,64},{64,7... | collective-permute-start | bytes 73736 | tf_op jit(solution)/shard_map/ppermute | solution.py:11
  93.2 2.1 %collective-permute-start.11 = (bf16[16,768]{1,0:T(8,128)(2,1)S(1)}, bf16[16,768]{1,0:T(8,128)(2,1)S(1)}, u32[]{:S(2)}, u32[]{:S(2)}) collective-permute-start(bf16[16,768]{1,0:T(8,128)(2,1)S(1)} %fusion.26), channel_id=1, source_target_pairs={{0,7},{1,0},{2,1},{3,2},{4,3},{5,4},{6,5},{7,6},{8,15},{9,8},{10,9... | collective-permute-start | bytes 73736 | tf_op jit(solution)/shard_map/ppermute | solution.py:11
  95.3 4.4 %collective-permute-start.10 = (bf16[16,768]{1,0:T(8,128)(2,1)S(1)}, bf16[16,768]{1,0:T(8,128)(2,1)S(1)}, u32[]{:S(2)}, u32[]{:S(2)}) collective-permute-start(bf16[16,768]{1,0:T(8,128)(2,1)S(1)} %fusion.26), channel_id=1, source_target_pairs={{0,1},{1,2},{2,3},{3,4},{4,5},{5,6},{6,7},{7,0},{8,9},{9,10},{10,1... | collective-permute-start | bytes 73736 | tf_op jit(solution)/shard_map/ppermute | solution.py:11
  99.7 7.6 %collective-permute-start.9 = (bf16[16,768]{1,0:T(8,128)(2,1)S(1)}, bf16[16,768]{1,0:T(8,128)(2,1)}, u32[]{:S(2)}, u32[]{:S(2)}) collective-permute-start(bf16[16,768]{1,0:T(8,128)(2,1)S(1)} %fusion.26), channel_id=1, source_target_pairs={{0,504},{8,0},{16,8},{24,16},{32,24},{40,32},{48,40},{56,48},{64,5... | collective-permute-start | bytes 73736 | tf_op jit(solution)/shard_map/ppermute | solution.py:11
  115.1 12.6 %all_to_all.22 = bf16[8,2,256]{2,1,0:T(2,128)(2,1)S(1)} all-to-all(bf16[8,2,256]{2,1,0:T(2,128)(2,1)S(1)} %reshape.221), channel_id=1, replica_groups=mesh['group'=64,'member'=8] {'member'}, dimensions={0} | all-to-all | bytes 16384 | tf_op jit(solution)/shard_map/all_to_all | solution.py:43
  128.5 1.7 convolution_bitcast_fusion
  131.4 1.3 reshape.223
  132.7 16.9 %all_to_all.23 = f32[64,1,512]{2,1,0:T(1,128)S(1)} all-to-all(f32[64,1,512]{2,1,0:T(1,128)S(1)} %reshape.223), channel_id=1, replica_groups=mesh['group'=64,'member'=8] {'group'}, dimensions={0} | all-to-all | bytes 262144 | tf_op jit(solution)/shard_map/all_to_all | solution.py:48
  152.7 1.9 %fusion.38 = (bf16[16,768]{1,0:T(8,128)(2,1)S(1)}, f32[16,768]{1,0:T(8,128)}) fusion(f32[16,768]{1,0:T(8,128)} %get-tuple-element.18, f32[16,768]{1,0:T(8,128)S(1)} %fusion.29, bf16[16,1024]{1,0:T(8,128)(2,1)S(1)} %concatenate.14, bf16[1,768,1024]{2,1,0:T(8,128)(2,1)S(1)} %copy-done), kind=kOutput, calls=%fused_computation.73 | convolution fusion | flops 25202688 | bytes 1777664 | tf_op jit(solution)/shard_map/cn,un->cu/dot_general | solution.py:50
  154.6 2.4 %collective-permute-start.12 = (bf16[16,768]{1,0:T(8,128)(2,1)S(1)}, bf16[16,768]{1,0:T(8,128)(2,1)S(1)}, u32[]{:S(2)}, u32[]{:S(2)}) collective-permute-start(bf16[16,768]{1,0:T(8,128)(2,1)S(1)} %get-tuple-element.19), channel_id=1, source_target_pairs={{0,8},{8,16},{16,24},{24,32},{32,40},{40,48},{48,56},{56,64},{64,7... | collective-permute-start | bytes 73736 | tf_op jit(solution)/shard_map/ppermute | solution.py:11
  157.0 7.1 %collective-permute-start.13 = (bf16[16,768]{1,0:T(8,128)(2,1)S(1)}, bf16[16,768]{1,0:T(8,128)(2,1)S(1)}, u32[]{:S(2)}, u32[]{:S(2)}) collective-permute-start(bf16[16,768]{1,0:T(8,128)(2,1)S(1)} %get-tuple-element.19), channel_id=1, source_target_pairs={{0,504},{8,0},{16,8},{24,16},{32,24},{40,32},{48,40},{56,48},{64,5... | collective-permute-start | bytes 73736 | tf_op jit(solution)/shard_map/ppermute | solution.py:11
  164.1 4.8 %collective-permute-start.14 = (bf16[16,768]{1,0:T(8,128)(2,1)S(1)}, bf16[16,768]{1,0:T(8,128)(2,1)S(1)}, u32[]{:S(2)}, u32[]{:S(2)}) collective-permute-start(bf16[16,768]{1,0:T(8,128)(2,1)S(1)} %get-tuple-element.19), channel_id=1, source_target_pairs={{0,1},{1,2},{2,3},{3,4},{4,5},{5,6},{6,7},{7,0},{8,9},{9,10},{10,1... | collective-permute-start | bytes 73736 | tf_op jit(solution)/shard_map/ppermute | solution.py:11
  168.9 1.9 %collective-permute-start.15 = (bf16[16,768]{1,0:T(8,128)(2,1)S(1)}, bf16[16,768]{1,0:T(8,128)(2,1)S(1)}, u32[]{:S(2)}, u32[]{:S(2)}) collective-permute-start(bf16[16,768]{1,0:T(8,128)(2,1)S(1)} %get-tuple-element.19), channel_id=1, source_target_pairs={{0,7},{1,0},{2,1},{3,2},{4,3},{5,4},{6,5},{7,6},{8,15},{9,8},{10,9... | collective-permute-start | bytes 73736 | tf_op jit(solution)/shard_map/ppermute | solution.py:11
  (151 shorter events, 37.9 us)
Async XLA Ops:
  0.6 65.5 %copy-start = (bf16[1,768,1024]{2,1,0:T(8,128)(2,1)S(1)}, bf16[1,768,1024]{2,1,0:T(8,128)(2,1)}, u32[]{:S(2)}) copy-start(bf16[1,768,1024]{2,1,0:T(8,128)(2,1)} %param.10) | copy-start | bytes 4718596
  0.6 49.1 %copy-start.2 = (bf16[32,64,256]{2,1,0:T(8,128)(2,1)S(1)}, bf16[32,64,256]{2,1,0:T(8,128)(2,1)}, u32[]{:S(2)}) copy-start(bf16[32,64,256]{2,1,0:T(8,128)(2,1)} %param.13) | copy-start | bytes 3145732
  1.6 32.9 %collective-permute-start.3 = (bf16[16,768]{1,0:T(8,128)(2,1)S(1)}, bf16[16,768]{1,0:T(8,128)(2,1)S(1)}, u32[]{:S(2)}, u32[]{:S(2)}) collective-permute-start(bf16[16,768]{1,0:T(8,128)(2,1)S(1)} %bitcast_convert_fusion), channel_id=1, source_target_pairs={{0,7},{1,0},{2,1},{3,2},{4,3},{5,4},{6,5},{7,6},{8,15},{9,8},{10,9... | collective-permute-start | bytes 73736 | tf_op jit(solution)/shard_map/ppermute | solution.py:11
  10.4 23.2 %collective-permute-start.2 = (bf16[16,768]{1,0:T(8,128)(2,1)S(1)}, bf16[16,768]{1,0:T(8,128)(2,1)S(1)}, u32[]{:S(2)}, u32[]{:S(2)}) collective-permute-start(bf16[16,768]{1,0:T(8,128)(2,1)S(1)} %bitcast_convert_fusion), channel_id=1, source_target_pairs={{0,1},{1,2},{2,3},{3,4},{4,5},{5,6},{6,7},{7,0},{8,9},{9,10},{10,1... | collective-permute-start | bytes 73736 | tf_op jit(solution)/shard_map/ppermute | solution.py:11
  12.3 20.4 %collective-permute-start.1 = (bf16[16,768]{1,0:T(8,128)(2,1)S(1)}, bf16[16,768]{1,0:T(8,128)(2,1)S(1)}, u32[]{:S(2)}, u32[]{:S(2)}) collective-permute-start(bf16[16,768]{1,0:T(8,128)(2,1)S(1)} %bitcast_convert_fusion), channel_id=1, source_target_pairs={{0,504},{8,0},{16,8},{24,16},{32,24},{40,32},{48,40},{56,48},{64,5... | collective-permute-start | bytes 73736 | tf_op jit(solution)/shard_map/ppermute | solution.py:11
  23.0 8.8 %collective-permute-start = (bf16[16,768]{1,0:T(8,128)(2,1)S(1)}, bf16[16,768]{1,0:T(8,128)(2,1)S(1)}, u32[]{:S(2)}, u32[]{:S(2)}) collective-permute-start(bf16[16,768]{1,0:T(8,128)(2,1)S(1)} %bitcast_convert_fusion), channel_id=1, source_target_pairs={{0,8},{8,16},{16,24},{24,32},{32,40},{40,48},{48,56},{56,64},{64,7... | collective-permute-start | bytes 73736 | tf_op jit(solution)/shard_map/ppermute | solution.py:11
  25.8 24.8 %copy-start.5 = (pred[64]{0:T(512)(128)(4,1)}, pred[64]{0:T(512)(128)(4,1)S(1)}, u32[]{:S(2)}) copy-start(pred[64]{0:T(512)(128)(4,1)S(1)} %get-tuple-element.3) | copy-start | bytes 196
  25.8 24.8 %copy-start.7 = (pred[64]{0:T(512)(128)(4,1)}, pred[64]{0:T(512)(128)(4,1)S(1)}, u32[]{:S(2)}) copy-start(pred[64]{0:T(512)(128)(4,1)S(1)} %get-tuple-element.15) | copy-start | bytes 196
  25.8 59.1 %copy-start.11 = (pred[64]{0:T(512)(128)(4,1)}, pred[64]{0:T(512)(128)(4,1)S(1)}, u32[]{:S(2)}) copy-start(pred[64]{0:T(512)(128)(4,1)S(1)} %get-tuple-element.13) | copy-start | bytes 196
  25.9 58.3 %copy-start.17 = (s32[1024]{0:T(1024)}, s32[1024]{0:T(1024)S(1)}, u32[]{:S(2)}) copy-start(s32[1024]{0:T(1024)S(1)} %pad_clamp_fusion.3) | copy-start | bytes 12292
  65.9 24.9 %copy-start.1 = (bf16[1,768,1024]{2,1,0:T(8,128)(2,1)S(1)}, bf16[1,768,1024]{2,1,0:T(8,128)(2,1)}, u32[]{:S(2)}) copy-start(bf16[1,768,1024]{2,1,0:T(8,128)(2,1)} %param.9) | copy-start | bytes 4718596
  65.9 24.9 %copy-start.4 = (f32[1,16,768]{2,1,0:T(8,128)S(1)}, f32[1,16,768]{2,1,0:T(8,128)}, u32[]{:S(2)}) copy-start(f32[1,16,768]{2,1,0:T(8,128)} %param.8) | copy-start | bytes 147460
  67.2 16.1 %collective-permute-start.4 = (bf16[16,768]{1,0:T(8,128)(2,1)S(1)}, bf16[16,768]{1,0:T(8,128)(2,1)}, u32[]{:S(2)}, u32[]{:S(2)}) collective-permute-start(bf16[16,768]{1,0:T(8,128)(2,1)S(1)} %get-tuple-element.17), channel_id=1, source_target_pairs={{0,8},{8,16},{16,24},{24,32},{32,40},{40,48},{48,56},{56,64},{64,7... | collective-permute-start | bytes 73736 | tf_op jit(solution)/shard_map/ppermute | solution.py:11
  69.7 19.3 %collective-permute-start.7 = (bf16[16,768]{1,0:T(8,128)(2,1)S(1)}, bf16[16,768]{1,0:T(8,128)(2,1)S(1)}, u32[]{:S(2)}, u32[]{:S(2)}) collective-permute-start(bf16[16,768]{1,0:T(8,128)(2,1)S(1)} %get-tuple-element.17), channel_id=1, source_target_pairs={{0,7},{1,0},{2,1},{3,2},{4,3},{5,4},{6,5},{7,6},{8,15},{9,8},{10,9... | collective-permute-start | bytes 73736 | tf_op jit(solution)/shard_map/ppermute | solution.py:11
  73.9 13.5 %collective-permute-start.6 = (bf16[16,768]{1,0:T(8,128)(2,1)S(1)}, bf16[16,768]{1,0:T(8,128)(2,1)S(1)}, u32[]{:S(2)}, u32[]{:S(2)}) collective-permute-start(bf16[16,768]{1,0:T(8,128)(2,1)S(1)} %get-tuple-element.17), channel_id=1, source_target_pairs={{0,1},{1,2},{2,3},{3,4},{4,5},{5,6},{6,7},{7,0},{8,9},{9,10},{10,1... | collective-permute-start | bytes 73736 | tf_op jit(solution)/shard_map/ppermute | solution.py:11
  76.2 8.7 %collective-permute-start.5 = (bf16[16,768]{1,0:T(8,128)(2,1)S(1)}, bf16[16,768]{1,0:T(8,128)(2,1)}, u32[]{:S(2)}, u32[]{:S(2)}) collective-permute-start(bf16[16,768]{1,0:T(8,128)(2,1)S(1)} %get-tuple-element.17), channel_id=1, source_target_pairs={{0,504},{8,0},{16,8},{24,16},{32,24},{40,32},{48,40},{56,48},{64,5... | collective-permute-start | bytes 73736 | tf_op jit(solution)/shard_map/ppermute | solution.py:11
  91.3 16.0 %collective-permute-start.8 = (bf16[16,768]{1,0:T(8,128)(2,1)S(1)}, bf16[16,768]{1,0:T(8,128)(2,1)}, u32[]{:S(2)}, u32[]{:S(2)}) collective-permute-start(bf16[16,768]{1,0:T(8,128)(2,1)S(1)} %fusion.26), channel_id=1, source_target_pairs={{0,8},{8,16},{16,24},{24,32},{32,40},{40,48},{48,56},{56,64},{64,7... | collective-permute-start | bytes 73736 | tf_op jit(solution)/shard_map/ppermute | solution.py:11
  93.2 19.9 %collective-permute-start.11 = (bf16[16,768]{1,0:T(8,128)(2,1)S(1)}, bf16[16,768]{1,0:T(8,128)(2,1)S(1)}, u32[]{:S(2)}, u32[]{:S(2)}) collective-permute-start(bf16[16,768]{1,0:T(8,128)(2,1)S(1)} %fusion.26), channel_id=1, source_target_pairs={{0,7},{1,0},{2,1},{3,2},{4,3},{5,4},{6,5},{7,6},{8,15},{9,8},{10,9... | collective-permute-start | bytes 73736 | tf_op jit(solution)/shard_map/ppermute | solution.py:11
  95.3 16.1 %collective-permute-start.10 = (bf16[16,768]{1,0:T(8,128)(2,1)S(1)}, bf16[16,768]{1,0:T(8,128)(2,1)S(1)}, u32[]{:S(2)}, u32[]{:S(2)}) collective-permute-start(bf16[16,768]{1,0:T(8,128)(2,1)S(1)} %fusion.26), channel_id=1, source_target_pairs={{0,1},{1,2},{2,3},{3,4},{4,5},{5,6},{6,7},{7,0},{8,9},{9,10},{10,1... | collective-permute-start | bytes 73736 | tf_op jit(solution)/shard_map/ppermute | solution.py:11
  99.7 9.4 %collective-permute-start.9 = (bf16[16,768]{1,0:T(8,128)(2,1)S(1)}, bf16[16,768]{1,0:T(8,128)(2,1)}, u32[]{:S(2)}, u32[]{:S(2)}) collective-permute-start(bf16[16,768]{1,0:T(8,128)(2,1)S(1)} %fusion.26), channel_id=1, source_target_pairs={{0,504},{8,0},{16,8},{24,16},{32,24},{40,32},{48,40},{56,48},{64,5... | collective-permute-start | bytes 73736 | tf_op jit(solution)/shard_map/ppermute | solution.py:11
  154.6 16.2 %collective-permute-start.12 = (bf16[16,768]{1,0:T(8,128)(2,1)S(1)}, bf16[16,768]{1,0:T(8,128)(2,1)S(1)}, u32[]{:S(2)}, u32[]{:S(2)}) collective-permute-start(bf16[16,768]{1,0:T(8,128)(2,1)S(1)} %get-tuple-element.19), channel_id=1, source_target_pairs={{0,8},{8,16},{16,24},{24,32},{32,40},{40,48},{48,56},{56,64},{64,7... | collective-permute-start | bytes 73736 | tf_op jit(solution)/shard_map/ppermute | solution.py:11
  157.0 14.8 %collective-permute-start.13 = (bf16[16,768]{1,0:T(8,128)(2,1)S(1)}, bf16[16,768]{1,0:T(8,128)(2,1)S(1)}, u32[]{:S(2)}, u32[]{:S(2)}) collective-permute-start(bf16[16,768]{1,0:T(8,128)(2,1)S(1)} %get-tuple-element.19), channel_id=1, source_target_pairs={{0,504},{8,0},{16,8},{24,16},{32,24},{40,32},{48,40},{56,48},{64,5... | collective-permute-start | bytes 73736 | tf_op jit(solution)/shard_map/ppermute | solution.py:11
  164.1 8.7 %collective-permute-start.14 = (bf16[16,768]{1,0:T(8,128)(2,1)S(1)}, bf16[16,768]{1,0:T(8,128)(2,1)S(1)}, u32[]{:S(2)}, u32[]{:S(2)}) collective-permute-start(bf16[16,768]{1,0:T(8,128)(2,1)S(1)} %get-tuple-element.19), channel_id=1, source_target_pairs={{0,1},{1,2},{2,3},{3,4},{4,5},{5,6},{6,7},{7,0},{8,9},{9,10},{10,1... | collective-permute-start | bytes 73736 | tf_op jit(solution)/shard_map/ppermute | solution.py:11
  168.9 6.1 %collective-permute-start.15 = (bf16[16,768]{1,0:T(8,128)(2,1)S(1)}, bf16[16,768]{1,0:T(8,128)(2,1)S(1)}, u32[]{:S(2)}, u32[]{:S(2)}) collective-permute-start(bf16[16,768]{1,0:T(8,128)(2,1)S(1)} %get-tuple-element.19), channel_id=1, source_target_pairs={{0,7},{1,0},{2,1},{3,2},{4,3},{5,4},{6,5},{7,6},{8,15},{9,8},{10,9... | collective-permute-start | bytes 73736 | tf_op jit(solution)/shard_map/ppermute | solution.py:11
  (10 other events, 226.9 us)
